TPU v7x, 256 devices: a whole 4x4x8 slice. The times are simulated.
256 devices in a mesh: narrow: 8 (over x, z_lo), wide: 32 (over y, z_hi, core).
Axes of the slice: x: 4, y: 4, z: 8 (z_hi: 4, z_lo: 2; z = z_hi * 2 + z_lo), core: 2. Of those that a mesh axis runs over, the one named last changes fastest.
Arguments:
- basis: bfloat16 [128, 32, 512, 128], P(None, 'narrow', 'wide'), may hold values from -6 to 6
- rhs: bfloat16 [32, 512, 128], P('narrow', 'wide'), may hold values from -48 to 48
- coeffs: float32 [4, 32, 512, 128], P(None, 'narrow', 'wide'), may hold values from 0.25 to 4
- rows: int32 [4, 32, 512, 128], P(None, 'narrow', 'wide'), may hold values from 0 to 255
- signs: int32 [4, 32, 512, 128], P(None, 'narrow', 'wide'), may hold values from 0 to 1
- params: float32 [256, 4], P(('narrow', 'wide')), may hold values from 0.25 to 4
- order: int32 [256], replicated, may hold values from 0 to 255, each once
Outputs:
- fields: bfloat16 [256, 32, 512, 128], P(None, 'narrow', 'wide')
Inputs may be any that keep to these rules, and one draw needn't show every extreme that they name: `order`: each point number appears exactly once.
All inputs are finite; a program needn't handle non-finite values.
Results may differ from a plain program's by a relative error of at most 0.0056.
Values may be sent and summed in bfloat16 or wider, within the bound.
No kernel may reach another device: no remote copies, remote signals or barrier semaphores. Data moves between devices by JAX's collectives and lax.ppermute only.
A program may use at most 64 MiB of HBM per device.

v0:
```python
import jax
import jax.numpy as jnp
from jax import lax
from jax.sharding import PartitionSpec as P

K = 128
M = 1024
TERMS = 4
NNZ = 4


def extended(cells, sides, width):
    for axis, dim in sides:
        count = lax.axis_size(axis)
        ends = count - 1
        head = lax.slice_in_dim(cells, 0, width, axis=dim)
        tail = lax.slice_in_dim(cells, cells.shape[dim] - width, cells.shape[dim], axis=dim)
        cells = jnp.concatenate(
            [
                lax.ppermute(tail, axis, [(i, (i + 1) % count) for i in range(ends)]),
                cells,
                lax.ppermute(head, axis, [((i + 1) % count, i) for i in range(ends)]),
            ],
            axis=dim,
        )
    return cells


def column_products(sketched, sketched_rhs):
    dims = (((0,), (0,)), ((), ()))
    gram_matrix = lax.dot_general(
        sketched,
        sketched,
        dims,
        precision=lax.Precision.HIGHEST,
        preferred_element_type=jnp.float32,
    )
    projected = lax.dot_general(
        sketched,
        sketched_rhs,
        dims,
        precision=lax.Precision.HIGHEST,
        preferred_element_type=jnp.float32,
    )
    return (gram_matrix, projected)


def solve_points(point_params, gram_matrix, projected):
    gram_blocks = gram_matrix.reshape(TERMS, K, TERMS, K)
    proj_blocks = projected.reshape(TERMS, K)
    pair_weight = point_params[:, :, None] * point_params[:, None, :]
    normal = jnp.einsum("pqr,qirj->pij", pair_weight, gram_blocks, precision=lax.Precision.HIGHEST)
    right_side = jnp.einsum("pq,qi->pi", point_params, proj_blocks, precision=lax.Precision.HIGHEST)
    lower_factor = jnp.linalg.cholesky(normal)
    forward = lax.linalg.triangular_solve(
        lower_factor, right_side[:, :, None], left_side=True, lower=True
    )
    solved = lax.linalg.triangular_solve(
        lower_factor, forward, left_side=True, lower=True, transpose_a=True
    )
    return solved[:, :, 0]


def per_device(basis, rhs, coeffs, rows, signs, params, order):
    cell_count = basis.shape[1] * basis.shape[2] * basis.shape[3]
    padded = extended(basis, (("narrow", 1), ("wide", 2)), 1).astype(jnp.float32)
    centre = padded[:, 1:-1, 1:-1, :]
    along_x = 2.0 * centre - padded[:, :-2, 1:-1, :] - padded[:, 2:, 1:-1, :]
    along_y = 2.0 * centre - padded[:, 1:-1, :-2, :] - padded[:, 1:-1, 2:, :]
    z_padded = jnp.pad(centre, ((0, 0), (0, 0), (0, 0), (1, 1)))
    along_z = 2.0 * centre - z_padded[..., :-2] - z_padded[..., 2:]
    terms = jnp.stack(
        [coeffs[0] * centre, coeffs[1] * along_x, coeffs[2] * along_y, coeffs[3] * along_z]
    )
    terms = terms.astype(jnp.bfloat16).reshape(TERMS * K, cell_count)
    row_block = M // NNZ
    flat_rows = rows.reshape(NNZ, cell_count)
    sign_values = ((2 * signs - 1).astype(jnp.float32) * 0.5).reshape(NNZ, cell_count)
    flat_rhs = rhs.reshape(cell_count)
    block_cells = max(min(1024, cell_count), cell_count // 16)
    block_count = cell_count // block_cells
    row_slots = lax.broadcasted_iota(jnp.int32, (1, row_block, 1), 1)

    def accumulate(turn_index, carry):
        sketch_sum, rhs_sum = carry
        offset = turn_index * block_cells
        hashed_rows = lax.dynamic_slice_in_dim(flat_rows, offset, block_cells, 1)
        hashed_signs = lax.dynamic_slice_in_dim(sign_values, offset, block_cells, 1)
        hashed = jnp.where(row_slots == hashed_rows[:, None, :], hashed_signs[:, None, :], 0.0)
        hashed = hashed.astype(jnp.bfloat16).reshape(M, block_cells)
        columns = lax.dynamic_slice_in_dim(terms, offset, block_cells, 1)
        sketch_sum = sketch_sum + lax.dot_general(
            hashed, columns, (((1,), (1,)), ((), ())), preferred_element_type=jnp.float32
        )
        source = lax.dynamic_slice_in_dim(flat_rhs, offset, block_cells, 0)
        rhs_sum = rhs_sum + jnp.dot(hashed, source, preferred_element_type=jnp.float32)
        return (sketch_sum, rhs_sum)

    start = (jnp.zeros((M, TERMS * K), jnp.float32), jnp.zeros((M,), jnp.float32))
    sketched, sketched_rhs = lax.fori_loop(0, block_count, accumulate, start)
    sketched, sketched_rhs = lax.psum((sketched, sketched_rhs), ("narrow", "wide"))
    gram_matrix, projected = column_products(sketched, sketched_rhs)
    own_coef = solve_points(params, gram_matrix, projected).astype(jnp.bfloat16)
    all_coef = lax.all_gather(own_coef, ("narrow", "wide"), axis=0, tiled=True)
    point_total = all_coef.shape[0]
    picker = (order[:, None] == lax.broadcasted_iota(jnp.int32, (1, point_total), 1)).astype(
        jnp.bfloat16
    )
    picked = jnp.dot(picker, all_coef, preferred_element_type=jnp.float32).astype(jnp.bfloat16)
    fields = jnp.dot(picked, basis.reshape(K, cell_count), preferred_element_type=jnp.float32)
    return fields.astype(jnp.bfloat16).reshape(
        point_total, basis.shape[1], basis.shape[2], basis.shape[3]
    )


def solution(mesh):
    in_specs = (
        P(None, "narrow", "wide", None),
        P("narrow", "wide", None),
        P(None, "narrow", "wide", None),
        P(None, "narrow", "wide", None),
        P(None, "narrow", "wide", None),
        P(("narrow", "wide"), None),
        P(),
    )
    out_specs = P(None, "narrow", "wide", None)
    return jax.shard_map(
        per_device, mesh=mesh, in_specs=in_specs, out_specs=out_specs, check_vma=False
    )
```

profile of v0, /device:TPU:1, one launch (start us, length us, event | category | flops | bytes accessed | tf_op | source)
XLA Modules:
  0.0 799.9 jit_solution(9524437281529108941)
XLA Ops:
  6.5 1.6 fusion.34
  9.0 5.1 collective-permute-start
  15.8 8.4 %collective-permute-done = bf16[128,1,16,128]{3,0,2,1:T(8,128)(2,1)} collective-permute-done((bf16[128,1,16,128]{3,0,2,1:T(8,128)(2,1)}, bf16[128,1,16,128]{3,0,2,1:T(8,128)(2,1)}, u32[]{:S(2)}, u32[]{:S(2)}) %collective-permute-start) | collective-permute-done | bytes 524320 | tf_op jit(solution)/shard_map/ppermute | solution.py:20
  25.4 1.5 constant_dynamic-update-slice_fusion.1
  26.9 10.0 %collective-permute-done.1 = bf16[128,1,16,128]{3,0,2,1:T(8,128)(2,1)S(1)} collective-permute-done((bf16[128,1,16,128]{3,0,2,1:T(8,128)(2,1)S(1)}, bf16[128,1,16,128]{3,0,2,1:T(8,128)(2,1)S(1)}, u32[]{:S(2)}, u32[]{:S(2)}) %collective-permute-start.1) | collective-permute-done | bytes 524320 | tf_op jit(solution)/shard_map/ppermute | solution.py:22
  37.0 6.3 collective-permute-start.2
  43.3 1.9 collective-permute-start.3
  46.0 7.4 collective-permute-done.3
  53.9 3.1 fusion.14
  57.0 2.2 fusion.19
  59.2 3.8 pad_maximum_fusion
  63.0 12.0 %copy.17 = bf16[4,128,4,16,128]{4,3,2,1,0:T(8,128)(2,1)} copy(bf16[4,128,4,16,128]{4,1,3,2,0:T(8,128)(2,1)} %pad_maximum_fusion) | data formatting | bytes 16777216 | tf_op jit(solution)/shard_map/stack | solution.py:72
  75.1 13.3 %convert_element_type.36 = bf16[512,8192]{1,0:T(8,128)(2,1)} reshape(bf16[4,128,4,16,128]{4,3,2,1,0:T(8,128)(2,1)} %copy.17) | data formatting | bytes 16777216 | tf_op jit(solution)/shard_map/convert_element_type | solution.py:75
  88.4 50.1 %while.16 = (s32[]{:T(128)}, f32[1024,512]{1,0:T(8,128)}, f32[1024]{0:T(1024)S(1)}, s32[4,8192]{1,0:T(4,128)S(1)}, bf16[4,8192]{1,0:T(4,128)(2,1)S(1)}, /*index=...) while((s32[]{:T(128)}, f32[1024,512]{1,0:T(8,128)}, ...), condition=%wide.region_1.2_spmd.clone, body=%wide.region_0.1_spmd.clone.sunk | while | flops 1078986752 | bytes 11651254 | solution.py:100
  88.8 3.8 select_add_fusion.4
  94.5 4.5 select_add_fusion.4
  100.8 4.5 select_add_fusion.4
  107.2 4.5 select_add_fusion.4
  113.5 4.5 select_add_fusion.4
  119.9 4.5 select_add_fusion.4
  126.2 4.5 select_add_fusion.4
  132.6 4.5 select_add_fusion.4
  138.6 78.1 %psum.15 = f32[1024]{0:T(1024)S(1)} all-reduce(f32[1024]{0:T(1024)S(1)} %get-tuple-element.146), channel_id=1, replica_groups=mesh['narrow'=8,'wide'=32] {'narrow','wide'}, use_global_device_ids=true, to_apply=%region_5.6 | all-reduce | flops 1024 | bytes 8192 | tf_op jit(solution)/shard_map/psum | solution.py:101
  216.7 186.0 %all-reduce.3.cloned.1.call-done = f32[1024,512]{1,0:T(8,128)} async-done(((f32[1024,512]{1,0:T(8,128)}), f32[1024,512]{1,0:T(8,128)}) %all-reduce.3.cloned.1.call-update) | async-done | bytes 2097168 | tf_op jit(solution)/shard_map/psum | solution.py:101
  402.7 5.7 fusion.36
  409.7 2.7 convolution_bitcast_fusion
  412.7 11.7 %custom-call.9 = f32[1,128,128]{2,1,0:T(8,128)S(1)} custom-call(f32[1,128,128]{2,1,0:T(8,128)S(1)} %fusion.29), custom_call_target="Cholesky" | custom-call | tf_op jit(solution)/shard_map/jit(cholesky)/cholesky | solution.py:54
  425.7 9.8 %custom-call.10 = f32[1,1,128,128]{2,3,1,0:T(8,128)S(1)} custom-call(f32[1,1,128,128]{3,2,1,0:T(8,128)S(1)} %fusion.24), custom_call_target="InvertDiagBlocksLowerTriangular" | custom-call | tf_op jit(solution)/shard_map/triangular_solve | solution.py:58
  435.5 1.5 fusion.37
  437.5 344.6 %all-gather.1 = bf16[256,1,128]{2,1,0:T(2,128)(2,1)S(1)} all-gather(bf16[1,1,128]{2,1,0:T(2,128)(2,1)S(1)} %fusion.21), channel_id=2, replica_groups=mesh['narrow'=8,'wide'=32] {'narrow','wide'}, dimensions={0}, use_global_device_ids=true | all-gather | bytes 65792 | tf_op jit(solution)/shard_map/all_gather | solution.py:104
  782.1 5.6 fusion.13
  787.7 5.4 copy.27
  (113 shorter events, 22.5 us)
Async XLA Ops:
  6.5 18.8 %copy-start.1 = (bf16[128,4,16,128]{3,2,1,0:T(8,128)(2,1)S(1)}, bf16[128,4,16,128]{3,2,1,0:T(8,128)(2,1)}, u32[]{:S(2)}) copy-start(bf16[128,4,16,128]{3,2,1,0:T(8,128)(2,1)} %param.9) | copy-start | bytes 6291460
  6.5 9.1 %copy-start.2 = (s32[4,4,16,128]{3,2,1,0:T(8,128)S(1)}, s32[4,4,16,128]{3,2,1,0:T(8,128)}, u32[]{:S(2)}) copy-start(s32[4,4,16,128]{3,2,1,0:T(8,128)} %param.13) | copy-start | bytes 393220
  6.5 9.2 %copy-start.3 = (s32[4,4,16,128]{3,2,1,0:T(8,128)S(1)}, s32[4,4,16,128]{3,2,1,0:T(8,128)}, u32[]{:S(2)}) copy-start(s32[4,4,16,128]{3,2,1,0:T(8,128)} %param.12) | copy-start | bytes 393220
  6.5 396.1 %all-reduce.3.cloned.1.call-start = ((), (), s32[]{:S(2)}) async-start(), calls=%async_computation | async-start | bytes 4194304 | tf_op jit(solution)/shard_map/psum | solution.py:101
  9.0 15.3 %collective-permute-start = (bf16[128,1,16,128]{3,0,2,1:T(8,128)(2,1)}, bf16[128,1,16,128]{3,0,2,1:T(8,128)(2,1)}, u32[]{:S(2)}, u32[]{:S(2)}) collective-permute-start(bf16[128,1,16,128]{3,0,2,1:T(8,128)(2,1)} %copy.40), channel_id=1, source_target_pairs={{0,32},{32,64},{64,96},{96,128},{128,160},{160,192},{192,224},{1,3... | collective-permute-start | bytes 1572872 | tf_op jit(solution)/shard_map/ppermute | solution.py:20
  14.3 22.6 %collective-permute-start.1 = (bf16[128,1,16,128]{3,0,2,1:T(8,128)(2,1)S(1)}, bf16[128,1,16,128]{3,0,2,1:T(8,128)(2,1)S(1)}, u32[]{:S(2)}, u32[]{:S(2)}) collective-permute-start(bf16[128,1,16,128]{3,0,2,1:T(8,128)(2,1)S(1)} %copy.41), channel_id=1, source_target_pairs={{32,0},{64,32},{96,64},{128,96},{160,128},{192,160},{224,192},{33,... | collective-permute-start | bytes 1572872 | tf_op jit(solution)/shard_map/ppermute | solution.py:22
  25.4 19.9 %copy-start.4 = (f32[4,4,16,128]{3,2,1,0:T(8,128)S(1)}, f32[4,4,16,128]{3,2,1,0:T(8,128)}, u32[]{:S(2)}) copy-start(f32[4,4,16,128]{3,2,1,0:T(8,128)} %param.11) | copy-start | bytes 393220
  37.0 8.9 %collective-permute-start.2 = (bf16[128,6,1,128]{3,0,2,1:T(8,128)(2,1)S(1)}, bf16[128,6,1,128]{3,0,2,1:T(8,128)(2,1)S(1)}, u32[]{:S(2)}, u32[]{:S(2)}) collective-permute-start(bf16[128,6,1,128]{3,0,2,1:T(8,128)(2,1)S(1)} %get-tuple-element.191), channel_id=1, source_target_pairs={{0,1},{1,2},{2,3},{3,4},{4,5},{5,6},{6,7},{7,8},{8,9},{9,10},{10,1... | collective-permute-start | bytes 589832 | tf_op jit(solution)/shard_map/ppermute | solution.py:20
  43.3 10.0 %collective-permute-start.3 = (bf16[128,6,1,128]{3,0,2,1:T(8,128)(2,1)S(1)}, bf16[128,6,1,128]{3,0,2,1:T(8,128)(2,1)S(1)}, u32[]{:S(2)}, u32[]{:S(2)}) collective-permute-start(bf16[128,6,1,128]{3,0,2,1:T(8,128)(2,1)S(1)} %get-tuple-element.192), channel_id=1, source_target_pairs={{1,0},{2,1},{3,2},{4,3},{5,4},{6,5},{7,6},{8,7},{9,8},{10,9},{11,1... | collective-permute-start | bytes 589832 | tf_op jit(solution)/shard_map/ppermute | solution.py:22
  88.4 50.1 %copy-start.5 = (f32[1,4]{1,0:T(1,128)S(1)}, f32[1,4]{1,0:T(1,128)}, u32[]{:S(2)}) copy-start(f32[1,4]{1,0:T(1,128)} %param.14) | copy-start | bytes 52
  408.4 27.2 %copy-start = (f32[1024,512]{1,0:T(8,128)S(1)}, f32[1024,512]{1,0:T(8,128)}, u32[]{:S(2)}) copy-start(f32[1024,512]{1,0:T(8,128)} %all-reduce.3.cloned.1.call-done) | copy-start | bytes 6291460
  408.4 373.7 %copy-start.6 = (s32[256]{0:T(256)S(1)}, s32[256]{0:T(256)}, u32[]{:S(2)}) copy-start(s32[256]{0:T(256)} %param.15) | copy-start | bytes 3076
Sparse Core Ops, SparseCore 0:
  138.6 263.9 all-reduce.2
where the time goes:
time: 801 us; the launch traced here: 800 us
  blocking collectives  423 us (53%)
  waiting for transfers between devices  213 us (27%)
  matrix products  56.7 us (7%)
  local copies, waits for them, and re-layouts  43.4 us (5%)
  other arithmetic  36 us (4%)
  starting transfers between devices  14.7 us (2%)
  between operations  13.6 us (2%)
    all_gather x1, blocking collectives, per_device(): all_coef = lax.all_gather(own_coef, ('narrow', 'wide'), axis=0, tiled=True)  345 us
    psum x1, waiting for transfers between devices, per_device(): lax.psum((sketched, sketched_rhs), ('narrow', 'wide'))  186 us
    psum x1, blocking collectives, per_device(): lax.psum((sketched, sketched_rhs), ('narrow', 'wide'))  78.1 us
    dot_general x8, matrix products, accumulate(): lax.dot_general(hashed, columns, (((1,), (1,)), ((), ())), preferred_elem...  35.6 us
    ppermute x2, waiting for transfers between devices, extended(): lax.ppermute(head, axis, [((i + 1) % count, i) for i in range(ends)])  17.4 us
  transfers between devices with their start and end apart: 5, of which 5 were waited for; matrix products, arithmetic and copies ran while one was open for 0% of the time, Pallas kernels for 0%

commit v1 on v0

--- a/solution.py
+++ b/solution.py
@@ -101,7 +101,8 @@
     sketched, sketched_rhs = lax.psum((sketched, sketched_rhs), ("narrow", "wide"))
     gram_matrix, projected = column_products(sketched, sketched_rhs)
     own_coef = solve_points(params, gram_matrix, projected).astype(jnp.bfloat16)
-    all_coef = lax.all_gather(own_coef, ("narrow", "wide"), axis=0, tiled=True)
+    sent = jnp.stack([own_coef] * lax.axis_size(("narrow", "wide")))
+    all_coef = jnp.concatenate(lax.all_to_all(sent, ("narrow", "wide"), 0, 0), axis=0)
     point_total = all_coef.shape[0]
     picker = (order[:, None] == lax.broadcasted_iota(jnp.int32, (1, point_total), 1)).astype(
         jnp.bfloat16

time: 801 us -> 482 us (0.60)
  blocking collectives: 423 us -> 103 us
    all_gather x1 -> x0, blocking collectives: 345 us -> none  [per_device(): all_coef = lax.all_gather(own_coef, ('narrow', 'wide'), axis=0, tiled=True)]
    all_to_all x0 -> x1, blocking collectives: none -> 25 us  [per_device(): lax.all_to_all(sent, ('narrow', 'wide'), 0, 0)]
  transfers between devices with their start and end apart: 5 -> 5, of which waited for: 5 -> 5; matrix products, arithmetic and copies ran while one was open for 0% -> 1% of each run, Pallas kernels for 0% -> 0%
where the time goes in v1:
time: 482 us; the launch traced here: 480 us
  waiting for transfers between devices  213 us (44%)
  blocking collectives  103 us (21%)
  matrix products  56.7 us (12%)
  local copies, waits for them, and re-layouts  43.5 us (9%)
  other arithmetic  36 us (7%)
  starting transfers between devices  14.7 us (3%)
  between operations  13.7 us (3%)
    psum x1, waiting for transfers between devices, per_device(): lax.psum((sketched, sketched_rhs), ('narrow', 'wide'))  186 us
    psum x1, blocking collectives, per_device(): lax.psum((sketched, sketched_rhs), ('narrow', 'wide'))  78.1 us
    dot_general x8, matrix products, accumulate(): lax.dot_general(hashed, columns, (((1,), (1,)), ((), ())), preferred_elem...  35.6 us
    all_to_all x1, blocking collectives, per_device(): lax.all_to_all(sent, ('narrow', 'wide'), 0, 0)  25 us
    ppermute x2, waiting for transfers between devices, extended(): lax.ppermute(head, axis, [((i + 1) % count, i) for i in range(ends)])  17.4 us
    convert_element_type x1, local copies, waits for them, and re-layouts, per_device(): terms = terms.astype(jnp.bfloat16).reshape(TERMS * K, cell_count)  13.3 us
    another operation x3, other arithmetic, solve_points(): lower_factor = jnp.linalg.cholesky(normal)  12.4 us
    another operation x1, local copies, waits for them, and re-layouts, per_device(): jnp.stack([coeffs[0] * centre, coeffs[1] * along_x, coeffs[2] * along_y,...  12 us
  transfers between devices with their start and end apart: 5, of which 5 were waited for; matrix products, arithmetic and copies ran while one was open for 1% of the time, Pallas kernels for 0%

profile of v1, /device:TPU:1, one launch (start us, length us, event | category | flops | bytes accessed | tf_op | source)
XLA Modules:
  0.0 480.5 jit_solution(15964447661283054262)
XLA Ops:
  6.5 1.6 fusion.33
  9.0 5.1 %collective-permute-start = (bf16[128,1,16,128]{3,0,2,1:T(8,128)(2,1)}, bf16[128,1,16,128]{3,0,2,1:T(8,128)(2,1)}, u32[]{:S(2)}, u32[]{:S(2)}) collective-permute-start(bf16[128,1,16,128]{3,0,2,1:T(8,128)(2,1)} %copy.40), channel_id=1, source_target_pairs={{0,32},{32,64},{64,96},{96,128},{128,160},{160,192},{192,224},{1,3... | collective-permute-start | bytes 1572872 | tf_op jit(solution)/shard_map/ppermute | solution.py:20
  15.8 8.4 %collective-permute-done = bf16[128,1,16,128]{3,0,2,1:T(8,128)(2,1)} collective-permute-done((bf16[128,1,16,128]{3,0,2,1:T(8,128)(2,1)}, bf16[128,1,16,128]{3,0,2,1:T(8,128)(2,1)}, u32[]{:S(2)}, u32[]{:S(2)}) %collective-permute-start) | collective-permute-done | bytes 524320 | tf_op jit(solution)/shard_map/ppermute | solution.py:20
  25.4 1.5 constant_dynamic-update-slice_fusion.1
  26.9 10.0 %collective-permute-done.1 = bf16[128,1,16,128]{3,0,2,1:T(8,128)(2,1)S(1)} collective-permute-done((bf16[128,1,16,128]{3,0,2,1:T(8,128)(2,1)S(1)}, bf16[128,1,16,128]{3,0,2,1:T(8,128)(2,1)S(1)}, u32[]{:S(2)}, u32[]{:S(2)}) %collective-permute-start.1) | collective-permute-done | bytes 524320 | tf_op jit(solution)/shard_map/ppermute | solution.py:22
  37.0 6.3 %collective-permute-start.2 = (bf16[128,6,1,128]{3,0,2,1:T(8,128)(2,1)S(1)}, bf16[128,6,1,128]{3,0,2,1:T(8,128)(2,1)S(1)}, u32[]{:S(2)}, u32[]{:S(2)}) collective-permute-start(bf16[128,6,1,128]{3,0,2,1:T(8,128)(2,1)S(1)} %get-tuple-element.191), channel_id=1, source_target_pairs={{0,1},{1,2},{2,3},{3,4},{4,5},{5,6},{6,7},{7,8},{8,9},{9,10},{10,1... | collective-permute-start | bytes 589832 | tf_op jit(solution)/shard_map/ppermute | solution.py:20
  43.3 1.9 collective-permute-start.3
  46.0 7.4 %collective-permute-done.3 = bf16[128,6,1,128]{3,0,2,1:T(8,128)(2,1)S(1)} collective-permute-done((bf16[128,6,1,128]{3,0,2,1:T(8,128)(2,1)S(1)}, bf16[128,6,1,128]{3,0,2,1:T(8,128)(2,1)S(1)}, u32[]{:S(2)}, u32[]{:S(2)}) %collective-permute-start.3) | collective-permute-done | bytes 196640 | tf_op jit(solution)/shard_map/ppermute | solution.py:22
  53.9 3.1 fusion.14
  57.0 2.2 fusion.19
  59.2 3.8 pad_maximum_fusion
  63.0 12.0 %copy.17 = bf16[4,128,4,16,128]{4,3,2,1,0:T(8,128)(2,1)} copy(bf16[4,128,4,16,128]{4,1,3,2,0:T(8,128)(2,1)} %pad_maximum_fusion) | data formatting | bytes 16777216 | tf_op jit(solution)/shard_map/stack | solution.py:72
  75.1 13.3 %convert_element_type.34 = bf16[512,8192]{1,0:T(8,128)(2,1)} reshape(bf16[4,128,4,16,128]{4,3,2,1,0:T(8,128)(2,1)} %copy.17) | data formatting | bytes 16777216 | tf_op jit(solution)/shard_map/convert_element_type | solution.py:75
  88.4 50.1 %while.16 = (s32[]{:T(128)}, f32[1024,512]{1,0:T(8,128)}, f32[1024]{0:T(1024)S(1)}, s32[4,8192]{1,0:T(4,128)S(1)}, bf16[4,8192]{1,0:T(4,128)(2,1)S(1)}, /*index=...) while((s32[]{:T(128)}, f32[1024,512]{1,0:T(8,128)}, ...), condition=%wide.region_1.2_spmd.clone, body=%wide.region_0.1_spmd.clone.sunk | while | flops 1078986752 | bytes 11651254 | solution.py:100
  88.8 3.8 select_add_fusion.4
  94.5 4.5 select_add_fusion.4
  100.8 4.5 select_add_fusion.4
  107.2 4.5 select_add_fusion.4
  113.5 4.5 select_add_fusion.4
  119.9 4.5 select_add_fusion.4
  126.2 4.5 select_add_fusion.4
  132.6 4.5 select_add_fusion.4
  138.6 78.1 %psum.15 = f32[1024]{0:T(1024)S(1)} all-reduce(f32[1024]{0:T(1024)S(1)} %get-tuple-element.146), channel_id=1, replica_groups=mesh['narrow'=8,'wide'=32] {'narrow','wide'}, use_global_device_ids=true, to_apply=%region_5.6 | all-reduce | flops 1024 | bytes 8192 | tf_op jit(solution)/shard_map/psum | solution.py:101
  216.7 186.0 %all-reduce.3.cloned.1.call-done = f32[1024,512]{1,0:T(8,128)} async-done(((f32[1024,512]{1,0:T(8,128)}), f32[1024,512]{1,0:T(8,128)}) %all-reduce.3.cloned.1.call-update) | async-done | bytes 2097168 | tf_op jit(solution)/shard_map/psum | solution.py:101
  402.7 5.7 %fusion.35 = f32[512,512]{1,0:T(8,128)S(1)} fusion(f32[1024,512]{1,0:T(8,128)} %all-reduce.3.cloned.1.call-done), kind=kOutput, calls=%fused_computation.71 | convolution fusion | flops 3221225472 | bytes 3145728 | tf_op jit(solution)/shard_map/dot_general | solution.py:31
  409.7 2.7 convolution_bitcast_fusion
  412.7 11.7 %custom-call.9 = f32[1,128,128]{2,1,0:T(8,128)S(1)} custom-call(f32[1,128,128]{2,1,0:T(8,128)S(1)} %fusion.28), custom_call_target="Cholesky" | custom-call | tf_op jit(solution)/shard_map/jit(cholesky)/cholesky | solution.py:54
  425.7 9.8 %custom-call.10 = f32[1,1,128,128]{2,3,1,0:T(8,128)S(1)} custom-call(f32[1,1,128,128]{3,2,1,0:T(8,128)S(1)} %fusion.23), custom_call_target="InvertDiagBlocksLowerTriangular" | custom-call | tf_op jit(solution)/shard_map/triangular_solve | solution.py:58
  435.5 1.5 fusion.36
  437.6 25.0 %all_to_all.5 = bf16[256,1,128]{2,1,0:T(2,128)(2,1)S(1)} all-to-all(bf16[256,1,128]{2,1,0:T(2,128)(2,1)S(1)} %stack.22), channel_id=1, replica_groups=mesh['narrow'=8,'wide'=32] {'narrow','wide'}, dimensions={0} | all-to-all | bytes 131072 | tf_op jit(solution)/shard_map/all_to_all | solution.py:105
  462.6 5.6 %fusion.13 = bf16[32,8,64,128]{3,1,2,0:T(8,128)(2,1)} fusion(bf16[16,8,64,128]{3,2,1,0:T(8,128)(2,1)} %bitcast.124, s32[256]{0:T(256)S(1)} %copy-done.6, bf16[256,1,128]{2,1,0:T(2,128)(2,1)S(1)} %all_to_all.5), kind=kOutput, calls=%fused_computation.29 | convolution fusion | flops 555843584 | bytes 6358016 | tf_op jit(solution)/shard_map/dot_general | solution.py:111
  468.2 5.4 %copy.27 = bf16[32,8,64,128]{3,2,1,0:T(8,128)(2,1)} copy(bf16[32,8,64,128]{3,1,2,0:T(8,128)(2,1)} %fusion.13) | data formatting | bytes 8388608
  (114 shorter events, 22.7 us)
Async XLA Ops:
  6.5 18.8 %copy-start.1 = (bf16[128,4,16,128]{3,2,1,0:T(8,128)(2,1)S(1)}, bf16[128,4,16,128]{3,2,1,0:T(8,128)(2,1)}, u32[]{:S(2)}) copy-start(bf16[128,4,16,128]{3,2,1,0:T(8,128)(2,1)} %param.9) | copy-start | bytes 6291460
  6.5 9.1 %copy-start.2 = (s32[4,4,16,128]{3,2,1,0:T(8,128)S(1)}, s32[4,4,16,128]{3,2,1,0:T(8,128)}, u32[]{:S(2)}) copy-start(s32[4,4,16,128]{3,2,1,0:T(8,128)} %param.13) | copy-start | bytes 393220
  6.5 9.2 %copy-start.3 = (s32[4,4,16,128]{3,2,1,0:T(8,128)S(1)}, s32[4,4,16,128]{3,2,1,0:T(8,128)}, u32[]{:S(2)}) copy-start(s32[4,4,16,128]{3,2,1,0:T(8,128)} %param.12) | copy-start | bytes 393220
  6.5 396.1 %all-reduce.3.cloned.1.call-start = ((), (), s32[]{:S(2)}) async-start(), calls=%async_computation.1 | async-start | bytes 4194304 | tf_op jit(solution)/shard_map/psum | solution.py:101
  9.0 15.3 %collective-permute-start = (bf16[128,1,16,128]{3,0,2,1:T(8,128)(2,1)}, bf16[128,1,16,128]{3,0,2,1:T(8,128)(2,1)}, u32[]{:S(2)}, u32[]{:S(2)}) collective-permute-start(bf16[128,1,16,128]{3,0,2,1:T(8,128)(2,1)} %copy.40), channel_id=1, source_target_pairs={{0,32},{32,64},{64,96},{96,128},{128,160},{160,192},{192,224},{1,3... | collective-permute-start | bytes 1572872 | tf_op jit(solution)/shard_map/ppermute | solution.py:20
  14.3 22.6 %collective-permute-start.1 = (bf16[128,1,16,128]{3,0,2,1:T(8,128)(2,1)S(1)}, bf16[128,1,16,128]{3,0,2,1:T(8,128)(2,1)S(1)}, u32[]{:S(2)}, u32[]{:S(2)}) collective-permute-start(bf16[128,1,16,128]{3,0,2,1:T(8,128)(2,1)S(1)} %copy.41), channel_id=1, source_target_pairs={{32,0},{64,32},{96,64},{128,96},{160,128},{192,160},{224,192},{33,... | collective-permute-start | bytes 1572872 | tf_op jit(solution)/shard_map/ppermute | solution.py:22
  25.4 19.9 %copy-start.4 = (f32[4,4,16,128]{3,2,1,0:T(8,128)S(1)}, f32[4,4,16,128]{3,2,1,0:T(8,128)}, u32[]{:S(2)}) copy-start(f32[4,4,16,128]{3,2,1,0:T(8,128)} %param.11) | copy-start | bytes 393220
  37.0 8.9 %collective-permute-start.2 = (bf16[128,6,1,128]{3,0,2,1:T(8,128)(2,1)S(1)}, bf16[128,6,1,128]{3,0,2,1:T(8,128)(2,1)S(1)}, u32[]{:S(2)}, u32[]{:S(2)}) collective-permute-start(bf16[128,6,1,128]{3,0,2,1:T(8,128)(2,1)S(1)} %get-tuple-element.191), channel_id=1, source_target_pairs={{0,1},{1,2},{2,3},{3,4},{4,5},{5,6},{6,7},{7,8},{8,9},{9,10},{10,1... | collective-permute-start | bytes 589832 | tf_op jit(solution)/shard_map/ppermute | solution.py:20
  43.3 10.0 %collective-permute-start.3 = (bf16[128,6,1,128]{3,0,2,1:T(8,128)(2,1)S(1)}, bf16[128,6,1,128]{3,0,2,1:T(8,128)(2,1)S(1)}, u32[]{:S(2)}, u32[]{:S(2)}) collective-permute-start(bf16[128,6,1,128]{3,0,2,1:T(8,128)(2,1)S(1)} %get-tuple-element.192), channel_id=1, source_target_pairs={{1,0},{2,1},{3,2},{4,3},{5,4},{6,5},{7,6},{8,7},{9,8},{10,9},{11,1... | collective-permute-start | bytes 589832 | tf_op jit(solution)/shard_map/ppermute | solution.py:22
  88.4 50.1 %copy-start.5 = (f32[1,4]{1,0:T(1,128)S(1)}, f32[1,4]{1,0:T(1,128)}, u32[]{:S(2)}) copy-start(f32[1,4]{1,0:T(1,128)} %param.14) | copy-start | bytes 52
  408.4 27.2 %copy-start = (f32[1024,512]{1,0:T(8,128)S(1)}, f32[1024,512]{1,0:T(8,128)}, u32[]{:S(2)}) copy-start(f32[1024,512]{1,0:T(8,128)} %all-reduce.3.cloned.1.call-done) | copy-start | bytes 6291460
  408.4 54.3 %copy-start.6 = (s32[256]{0:T(256)S(1)}, s32[256]{0:T(256)}, u32[]{:S(2)}) copy-start(s32[256]{0:T(256)} %param.15) | copy-start | bytes 3076
Sparse Core Ops, SparseCore 0:
  138.6 263.9 all-reduce.2
